TPU v7x, 256 devices: a whole 4x4x8 slice. The times are simulated.
256 devices in a mesh: obs: 64 (over x, z, core), tile: 4 (over y).
Axes of the slice: x: 4, y: 4, z: 8, core: 2. Of those that a mesh axis runs over, the one named last changes fastest.
Arguments:
- jacobian: bfloat16 [16384, 65536], P(('obs', 'tile')), may hold values from -0.1875 to 0.1875
- obs_weight: float32 [16384], P(('obs', 'tile')), may hold values from 0.1 to 10
- block_order: int32 [512], replicated, may hold values from 0 to 511, each once
- tile_pairs: int32 [64, 64, 2], P('obs'), may hold values from 0 to 7, as said below
- tile_count: int32 [64], P('obs'), may hold values from 1 to 64, as said below
Outputs:
- hessian: float32 [4096, 128, 128], P(('obs', 'tile'))
Inputs may be any that keep to these rules, and one draw needn't show every extreme that they name: `tile_pairs`: slot numbers within an owner's own 8 slots; the first tile_count[j] pairs of owner j are distinct. `tile_count`: some owner has 64 live tiles.
All inputs are finite; a program needn't handle non-finite values.
Results may differ from a plain program's by a relative error of at most 0.0015.
Values may be sent and summed in bfloat16 or wider, within the bound.
No kernel may reach another device: no remote copies, remote signals or barrier semaphores. Data moves between devices by JAX's collectives and lax.ppermute only.
A program may use at most 256 MiB of HBM per device.

v0:
```python
import jax
import jax.numpy as jnp
from jax import lax
from jax.sharding import PartitionSpec as P

BLOCK = 128


def body(jacobian, obs_weight, block_order, tile_pairs, tile_count):
    row_count = jacobian.shape[0]
    owners = lax.axis_size("obs")
    total_blocks = block_order.shape[0]
    own_blocks = total_blocks // owners
    own_width = own_blocks * BLOCK
    blocks = jacobian.reshape(row_count, total_blocks, BLOCK)
    ordered = jnp.take(blocks, block_order, axis=1)
    root_weight = jnp.sqrt(obs_weight)[:, None, None]
    scaled = (ordered.astype(jnp.float32) * root_weight).astype(jnp.bfloat16)
    outgoing = scaled.reshape(row_count, owners, own_width)
    arrived = lax.all_to_all(outgoing, "obs", split_axis=1, concat_axis=0, tiled=True)
    columns = arrived.reshape(row_count * owners, own_width)
    pair_list = tile_pairs[0]
    live_count = tile_count[0]
    slot_total = pair_list.shape[0]
    slot_ids = jnp.arange(slot_total, dtype=jnp.int32)
    is_live = slot_ids < live_count
    per_group = min(own_blocks, 8)

    def gram_group(group_index, tiles):
        first_slot = group_index * per_group
        gram_part = lax.dot_general(
            columns, columns, (((0,), (0,)), ((), ())), preferred_element_type=jnp.float32
        )
        gram_tiles = gram_part.reshape(per_group, BLOCK, own_blocks, BLOCK).transpose(0, 2, 1, 3)
        gram_tiles = gram_tiles.reshape(per_group * own_blocks, BLOCK, BLOCK)
        relative = pair_list[:, 0] - first_slot
        inside = (relative >= 0) & (relative < per_group) & is_live
        lookup = jnp.clip(relative, 0, per_group - 1) * own_blocks + pair_list[:, 1]
        picked = jnp.take(gram_tiles, lookup, axis=0)
        return jnp.where(inside[:, None, None], picked, tiles)

    all_tiles = lax.fori_loop(
        0, own_blocks // per_group, gram_group, jnp.zeros((slot_total, BLOCK, BLOCK), jnp.float32)
    )
    hessian = lax.psum_scatter(all_tiles, "tile", scatter_dimension=0, tiled=True)
    return hessian


def solution(mesh):
    return jax.shard_map(
        body,
        mesh=mesh,
        in_specs=(
            P(("obs", "tile"), None),
            P(("obs", "tile")),
            P(),
            P("obs", None, None),
            P("obs"),
        ),
        out_specs=P(("obs", "tile"), None, None),
        check_vma=False,
    )
```

profile of v0, /device:TPU:1, one launch (start us, length us, event | category | flops | bytes accessed | tf_op | source)
XLA Modules:
  0.0 376.2 jit_solution(16123092588798176954)
XLA Ops:
  6.5 0.7 compare_select_fusion
  7.2 0.7 compare_and_fusion
  7.9 9.0 %copy_bitcast_fusion = bf16[64,512,128]{2,0,1:T(8,128)(2,1)} fusion(bf16[64,65536]{1,0:T(8,128)(2,1)} %param.5), kind=kLoop, calls=%fused_computation.3 | loop fusion | bytes 16777216 | tf_op jit(solution)/shard_map/reshape | solution.py:15
  16.9 23.0 %gather_fusion = bf16[512,64,128]{2,1,0:T(8,128)(2,1)} fusion(bf16[64,512,128]{2,0,1:T(8,128)(2,1)} %copy_bitcast_fusion, s32[1024]{0:T(1024)S(1)} %pad_clamp_fusion.1), kind=kCustom, calls=%fused_computation | custom fusion | bytes 16779264 | tf_op jit(solution)/shard_map/jit(_take)/gather | solution.py:16
  40.0 12.0 %copy.13 = bf16[64,512,128]{2,1,0:T(8,128)(2,1)} copy(bf16[64,512,128]{2,0,1:T(8,128)(2,1)} %bitcast.35) | data formatting | bytes 16777216 | tf_op jit(solution)/shard_map/jit(_take)/gather | solution.py:16
  52.0 0.0 copy-start.1
  52.0 13.3 %gather.12 = bf16[64,64,1024]{2,1,0:T(8,128)(2,1)} reshape(bf16[64,512,128]{2,1,0:T(8,128)(2,1)} %copy.13) | data formatting | bytes 16777216 | tf_op jit(solution)/shard_map/jit(_take)/gather | solution.py:16
  65.3 0.1 broadcast_in_dim.50
  65.4 0.1 broadcast_in_dim.51
  65.6 0.0 copy-done.1
  65.6 10.0 %multiply_convert_fusion = bf16[64,64,1024]{2,1,0:T(8,128)(2,1)} fusion(f32[64]{0:T(128)S(1)} %sqrt.3, bf16[64,64,1024]{2,1,0:T(8,128)(2,1)} %gather.12, pred[64,1024]{1,0:T(8,128)(4,1)S(1)} %bitcast.39), kind=kLoop, calls=%fused_computation.2 | loop fusion | flops 16777216 | bytes 16843008 | tf_op jit(solution)/shard_map/convert_element_type | solution.py:18
  75.6 11.3 %copy.14 = bf16[64,64,1024]{2,0,1:T(8,128)(2,1)} copy(bf16[64,64,1024]{2,1,0:T(8,128)(2,1)} %multiply_convert_fusion) | data formatting | bytes 16777216 | tf_op jit(solution)/shard_map/convert_element_type | solution.py:18
  86.9 0.0 copy-start
  86.9 13.3 %all-to-all-start = ((bf16[64,64,1024]{2,0,1:T(8,128)(2,1)}), bf16[64,64,1024]{2,0,1:T(8,128)(2,1)}, u32[]{:S(2)}, u32[]{:S(2)}) async-start(bf16[64,64,1024]{2,0,1:T(8,128)(2,1)} %copy.14), calls=%async_computation | async-start | bytes 16777216 | tf_op jit(solution)/shard_map/all_to_all | solution.py:20
  100.2 0.0 reduce-scatter.2.cloned.1.call-start
  100.9 0.0 copy-done
  100.9 185.0 %all-to-all-done = bf16[64,64,1024]{2,0,1:T(8,128)(2,1)} async-done(((bf16[64,64,1024]{2,0,1:T(8,128)(2,1)}), bf16[64,64,1024]{2,0,1:T(8,128)(2,1)}, u32[]{:S(2)}, u32[]{:S(2)}) %all-to-all-start) | async-done | bytes 8388640 | tf_op jit(solution)/shard_map/all_to_all | solution.py:20
  286.0 11.6 %copy.15 = bf16[1024,4096]{1,0:T(8,128)(2,1)} copy(bf16[1024,4096]{0,1:T(8,128)(2,1)} %bitcast.8) | data formatting | bytes 16777216 | tf_op jit(solution)/shard_map/while/body/eval_jaxpr/dot_general | solution.py:31
  297.5 15.9 %fusion = f32[8,128,8,128]{3,1,2,0:T(8,128)} fusion(bf16[8,128,4096,1]{2,1,3,0:T(8,128)(2,1)} %bitcast.36, bf16[8,128,4096,1]{2,1,0,3:T(8,128)(2,1)} %bitcast.37), kind=kOutput, calls=%fused_computation.13 | convolution fusion | flops 8589934592 | bytes 20971520 | tf_op jit(solution)/shard_map/while/body/eval_jaxpr/dot_general | solution.py:31
  313.4 5.0 %gather_fusion.1 = f32[64,128,128]{2,1,0:T(8,128)} fusion(f32[64,128,128]{2,1,0:T(8,128)} %bitcast.38, s32[1024]{0:T(1024)S(1)} %pad_clamp_fusion), kind=kCustom, calls=%fused_computation.1 | custom fusion | bytes 8388864 | tf_op jit(solution)/shard_map/while/body/eval_jaxpr/jit(_take)/gather | solution.py:39
  318.4 4.7 %select_select_fusion = f32[64,128,128]{2,1,0:T(8,128)} fusion(f32[64,128,128]{2,1,0:T(8,128)} %gather_fusion.1, pred[64]{0:T(512)(128)(4,1)S(1)} %get-tuple-element.15, pred[64]{0:T(512)(128)(4,1)S(1)} %bitcast_and_fusion), kind=kLoop, calls=%fused_computation.4 | loop fusion | flops 2097152 | bytes 8388736 | tf_op jit(solution)/shard_map/while/body/eval_jaxpr/jit(_where)/select_n | solution.py:40
  323.0 0.0 reduce-scatter.2.cloned.1.call-update
  323.0 46.3 %reduce-scatter.2.cloned.1.call-done = f32[16,128,128]{2,1,0:T(8,128)} async-done(((f32[64,128,128]{2,1,0:T(8,128)}), f32[16,128,128]{2,1,0:T(8,128)}) %reduce-scatter.2.cloned.1.call-update) | async-done | bytes 1048592 | tf_op jit(solution)/shard_map/reduce_scatter | solution.py:45
  (6 shorter events, 0.1 us)
Async XLA Ops:
  52.0 13.6 %copy-start.1 = (f32[64]{0:T(128)S(1)}, f32[64]{0:T(128)}, u32[]{:S(2)}) copy-start(f32[64]{0:T(128)} %param.6) | copy-start | bytes 772
  86.9 14.0 %copy-start = (s32[1,64,2]{1,2,0:T(2,128)S(1)}, s32[1,64,2]{1,2,0:T(2,128)}, u32[]{:S(2)}) copy-start(s32[1,64,2]{1,2,0:T(2,128)} %param.8) | copy-start | bytes 1540
  86.9 199.1 %all-to-all-start = ((bf16[64,64,1024]{2,0,1:T(8,128)(2,1)}), bf16[64,64,1024]{2,0,1:T(8,128)(2,1)}, u32[]{:S(2)}, u32[]{:S(2)}) async-start(bf16[64,64,1024]{2,0,1:T(8,128)(2,1)} %copy.14), calls=%async_computation | async-start | bytes 16777216 | tf_op jit(solution)/shard_map/all_to_all | solution.py:20
  100.2 269.2 %reduce-scatter.2.cloned.1.call-start = ((), (), s32[]{:S(2)}) async-start(), calls=%async_computation.2 | async-start | bytes 5242880 | tf_op jit(solution)/shard_map/reduce_scatter | solution.py:45
Sparse Core Ops, SparseCore 0:
  323.2 46.1 reduce-scatter.1
where the time goes:
time: 377 us; the launch traced here: 376 us
  waiting for transfers between devices  231 us (61%)
  local copies, waits for them, and re-layouts  85.5 us (23%)
  other arithmetic  16 us (4%)
  matrix products  15.9 us (4%)
  between operations  14.1 us (4%)
  starting transfers between devices  13.3 us (4%)
    all_to_all x1, waiting for transfers between devices, body(): lax.all_to_all(outgoing, 'obs', split_axis=1, concat_axis=0, tiled=True)  185 us
    gather x3, local copies, waits for them, and re-layouts, body(): ordered = jnp.take(blocks, block_order, axis=1)  48.4 us
    reduce_scatter x1, waiting for transfers between devices, body(): lax.psum_scatter(all_tiles, 'tile', scatter_dimension=0, tiled=True)  46.3 us
    dot_general x1, matrix products, gram_group(): lax.dot_general(columns, columns, (((0,), (0,)), ((), ())), preferred_ele...  15.9 us
    all_to_all x1, starting transfers between devices, body(): lax.all_to_all(outgoing, 'obs', split_axis=1, concat_axis=0, tiled=True)  13.3 us
    dot_general x1, local copies, waits for them, and re-layouts, gram_group(): lax.dot_general(columns, columns, (((0,), (0,)), ((), ())), preferred_ele...  11.6 us
    convert_element_type x1, local copies, waits for them, and re-layouts, body(): scaled = (ordered.astype(jnp.float32) * root_weight).astype(jnp.bfloat16)  11.3 us
    convert_element_type x1, other arithmetic, body(): scaled = (ordered.astype(jnp.float32) * root_weight).astype(jnp.bfloat16)  9.97 us
  transfers between devices with their start and end apart: 2, of which 2 were waited for; matrix products, arithmetic and copies ran while one was open for 0% of the time, Pallas kernels for 0%

commit v1 on v0

--- a/solution.py
+++ b/solution.py
@@ -17,7 +17,10 @@
     root_weight = jnp.sqrt(obs_weight)[:, None, None]
     scaled = (ordered.astype(jnp.float32) * root_weight).astype(jnp.bfloat16)
     outgoing = scaled.reshape(row_count, owners, own_width)
-    arrived = lax.all_to_all(outgoing, "obs", split_axis=1, concat_axis=0, tiled=True)
+    arrived = jnp.concatenate(
+        lax.all_to_all(jnp.stack(jnp.split(outgoing, lax.axis_size("obs"), axis=1)), "obs", 0, 0),
+        axis=0,
+    )
     columns = arrived.reshape(row_count * owners, own_width)
     pair_list = tile_pairs[0]
     live_count = tile_count[0]

time: 377 us -> 439 us (1.16)
  local copies, waits for them, and re-layouts: 85.5 us -> 147 us
    unnamed x5 -> x70, local copies, waits for them, and re-layouts: 0.04 us -> 43.7 us
    split x0 -> x4, local copies, waits for them, and re-layouts: none -> 28.3 us  [body(): jnp.split(outgoing, lax.axis_size('obs'), axis=1)]
    convert_element_type x1 -> x0, local copies, waits for them, and re-layouts: 11.3 us -> none  [body(): scaled = (ordered.astype(jnp.float32) * root_weight).astype(jnp.bfloat16)]
where the time goes in v1:
time: 439 us; the launch traced here: 438 us
  waiting for transfers between devices  231 us (53%)
  local copies, waits for them, and re-layouts  147 us (33%)
  other arithmetic  16.7 us (4%)
  matrix products  15.9 us (4%)
  between operations  14.2 us (3%)
  starting transfers between devices  13.3 us (3%)
    all_to_all x1, waiting for transfers between devices, body(): lax.all_to_all(jnp.stack(jnp.split(outgoing, lax.axis_size('obs'), axis=1...  185 us
    gather x3, local copies, waits for them, and re-layouts, body(): ordered = jnp.take(blocks, block_order, axis=1)  48.4 us
    reduce_scatter x1, waiting for transfers between devices, body(): lax.psum_scatter(all_tiles, 'tile', scatter_dimension=0, tiled=True)  46.3 us
    unnamed x70, local copies, waits for them, and re-layouts  43.7 us
    split x4, local copies, waits for them, and re-layouts, body(): jnp.split(outgoing, lax.axis_size('obs'), axis=1)  28.3 us
    dot_general x1, matrix products, gram_group(): lax.dot_general(columns, columns, (((0,), (0,)), ((), ())), preferred_ele...  15.9 us
    all_to_all x1, starting transfers between devices, body(): lax.all_to_all(jnp.stack(jnp.split(outgoing, lax.axis_size('obs'), axis=1...  13.3 us
    dot_general x1, local copies, waits for them, and re-layouts, gram_group(): lax.dot_general(columns, columns, (((0,), (0,)), ((), ())), preferred_ele...  11.3 us
  transfers between devices with their start and end apart: 2, of which 2 were waited for; matrix products, arithmetic and copies ran while one was open for 0% of the time, Pallas kernels for 0%

profile of v1, /device:TPU:1, one launch (start us, length us, event | category | flops | bytes accessed | tf_op | source)
XLA Modules:
  0.0 438.3 jit_solution(5040270233363908134)
XLA Ops:
  7.9 0.8 and_bitcast_fusion
  8.7 9.0 %copy_bitcast_fusion = bf16[64,512,128]{2,0,1:T(8,128)(2,1)} fusion(bf16[64,65536]{1,0:T(8,128)(2,1)} %param.5), kind=kLoop, calls=%fused_computation.3 | loop fusion | bytes 16777216 | tf_op jit(solution)/shard_map/reshape | solution.py:15
  17.7 23.0 %gather_fusion = bf16[512,64,128]{2,1,0:T(8,128)(2,1)} fusion(bf16[64,512,128]{2,0,1:T(8,128)(2,1)} %copy_bitcast_fusion, s32[1024]{0:T(1024)S(1)} %get-tuple-element.90), kind=kCustom, calls=%fused_computation | custom fusion | bytes 16779264 | tf_op jit(solution)/shard_map/jit(_take)/gather | solution.py:16
  40.8 12.0 %copy.1551 = bf16[64,512,128]{2,1,0:T(8,128)(2,1)} copy(bf16[64,512,128]{2,0,1:T(8,128)(2,1)} %bitcast.159) | data formatting | bytes 16777216 | tf_op jit(solution)/shard_map/jit(_take)/gather | solution.py:16
  52.8 13.4 %gather.12 = bf16[64,64,1024]{2,1,0:T(8,128)(2,1)} reshape(bf16[64,512,128]{2,1,0:T(8,128)(2,1)} %copy.1551) | data formatting | bytes 16777216 | tf_op jit(solution)/shard_map/jit(_take)/gather | solution.py:16
  66.4 10.0 %multiply_convert_fusion = bf16[64,64,1024]{2,1,0:T(8,128)(2,1)} fusion(f32[64]{0:T(128)S(1)} %sqrt.3, bf16[64,64,1024]{2,1,0:T(8,128)(2,1)} %gather.12, pred[64,1024]{1,0:T(8,128)(4,1)S(1)} %bitcast.163), kind=kLoop, calls=%fused_computation.2 | loop fusion | flops 16777216 | bytes 16843008 | tf_op jit(solution)/shard_map/convert_element_type | solution.py:18
  76.4 5.6 %fusion.3 = (bf16[64,1,1024]{2,1,0:T(2,128)(2,1)S(1)}, bf16[64,1,1024]{2,1,0:T(2,128)(2,1)S(1)}, bf16[64,1,1024]{2,1,0:T(2,128)(2,1)S(1)}, bf16[64,1,1024]{2,1,0...) fusion(bf16[64,64,1024]{2,1,0:T(8,128)(2,1)} %multiply_convert_, ...), kind=kLoop, calls=%fused_computation.80 | loop fusion | bytes 1835008 | tf_op jit(solution)/shard_map/split | solution.py:21
  82.0 11.9 %fusion.2 = (bf16[64,1,1024]{2,1,0:T(2,128)(2,1)S(1)}, bf16[64,1,1024]{2,1,0:T(2,128)(2,1)S(1)}, bf16[64,1,1024]{2,1,0:T(2,128)(2,1)S(1)}, bf16[64,1,1024]{2,1,0...) fusion(bf16[64,64,1024]{2,1,0:T(8,128)(2,1)} %multiply_convert_, ...), kind=kLoop, calls=%fused_computation.79 | loop fusion | bytes 4980736 | tf_op jit(solution)/shard_map/split | solution.py:21
  93.9 5.1 %fusion.1 = (bf16[64,1,1024]{2,1,0:T(2,128)(2,1)S(1)}, bf16[64,1,1024]{2,1,0:T(2,128)(2,1)S(1)}, bf16[64,1,1024]{2,1,0:T(2,128)(2,1)S(1)}, bf16[64,1,1024]{2,1,0...) fusion(bf16[64,64,1024]{2,1,0:T(8,128)(2,1)S(1)} %copy-done), kind=kLoop, calls=%fused_computation.78 | loop fusion | bytes 4980736 | tf_op jit(solution)/shard_map/split | solution.py:21
  99.0 5.7 %fusion = (bf16[64,1,1024]{2,1,0:T(2,128)(2,1)S(1)}, bf16[64,1,1024]{2,1,0:T(2,128)(2,1)S(1)}, bf16[64,1,1024]{2,1,0:T(2,128)(2,1)S(1)}, bf16[64,1,1024]{2,1,0:T...) fusion(bf16[64,64,1024]{2,1,0:T(8,128)(2,1)S(1)} %copy-done), kind=kLoop, calls=%fused_computation.77 | loop fusion | bytes 4980736 | tf_op jit(solution)/shard_map/split | solution.py:21
  117.9 0.7 constant_dynamic-update-slice_fusion.44
  122.1 0.7 constant_dynamic-update-slice_fusion.38
  128.3 0.7 constant_dynamic-update-slice_fusion.29
  135.2 0.7 constant_dynamic-update-slice_fusion.19
  137.3 0.7 constant_dynamic-update-slice_fusion.16
  138.0 0.7 constant_dynamic-update-slice_fusion.15
  145.6 0.7 constant_dynamic-update-slice_fusion.4
  149.1 13.3 %all-to-all-start = ((bf16[64,64,1,1024]{3,1,2,0:T(8,128)(2,1)}), bf16[64,64,1,1024]{3,1,2,0:T(8,128)(2,1)}, u32[]{:S(2)}, u32[]{:S(2)}) async-start(bf16[64,64,1,1024]{3,1,2,0:T(8,128)(2,1)} %constant_dynamic-update-slice_fusion), calls=%async_computation | async-start | bytes 16777216 | tf_op jit(solution)/shard_map/all_to_all | solution.py:21
  163.2 185.0 %all-to-all-done = bf16[64,64,1,1024]{3,1,2,0:T(8,128)(2,1)} async-done(((bf16[64,64,1,1024]{3,1,2,0:T(8,128)(2,1)}), bf16[64,64,1,1024]{3,1,2,0:T(8,128)(2,1)}, u32[]{:S(2)}, u32[]{:S(2)}) %all-to-all-start) | async-done | bytes 8388640 | tf_op jit(solution)/shard_map/all_to_all | solution.py:21
  348.2 11.3 %copy.1552 = bf16[1024,4096]{1,0:T(8,128)(2,1)} copy(bf16[1024,4096]{0,1:T(8,128)(2,1)} %bitcast.6) | data formatting | bytes 16777216 | tf_op jit(solution)/shard_map/while/body/eval_jaxpr/dot_general | solution.py:34
  359.5 15.9 %fusion.4 = f32[8,128,8,128]{3,1,2,0:T(8,128)} fusion(bf16[8,128,4096,1]{2,1,3,0:T(8,128)(2,1)} %bitcast.160, bf16[8,128,4096,1]{2,1,0,3:T(8,128)(2,1)} %bitcast.161), kind=kOutput, calls=%fused_computation.81 | convolution fusion | flops 8589934592 | bytes 20971520 | tf_op jit(solution)/shard_map/while/body/eval_jaxpr/dot_general | solution.py:34
  375.5 5.0 %gather_fusion.1 = f32[64,128,128]{2,1,0:T(8,128)} fusion(f32[64,128,128]{2,1,0:T(8,128)} %bitcast.162, s32[1024]{0:T(1024)S(1)} %get-tuple-element.89), kind=kCustom, calls=%fused_computation.1 | custom fusion | bytes 8388864 | tf_op jit(solution)/shard_map/while/body/eval_jaxpr/jit(_take)/gather | solution.py:42
  380.4 4.6 %select_select_fusion = f32[64,128,128]{2,1,0:T(8,128)} fusion(f32[64,128,128]{2,1,0:T(8,128)} %gather_fusion.1, pred[64]{0:T(512)(128)(4,1)S(1)} %get-tuple-element.15, pred[64]{0:T(512)(128)(4,1)S(1)} %bitcast_and_fusion), kind=kLoop, calls=%fused_computation.4 | loop fusion | flops 2097152 | bytes 8388736 | tf_op jit(solution)/shard_map/while/body/eval_jaxpr/jit(_where)/select_n | solution.py:43
  385.1 46.3 %reduce-scatter.2.cloned.1.call-done = f32[16,128,128]{2,1,0:T(8,128)} async-done(((f32[64,128,128]{2,1,0:T(8,128)}), f32[16,128,128]{2,1,0:T(8,128)}) %reduce-scatter.2.cloned.1.call-update) | async-done | bytes 1048592 | tf_op jit(solution)/shard_map/reduce_scatter | solution.py:48
  (73 shorter events, 41.1 us)
Async XLA Ops:
  52.8 13.7 %copy-start.2 = (f32[64]{0:T(128)S(1)}, f32[64]{0:T(128)}, u32[]{:S(2)}) copy-start(f32[64]{0:T(128)} %param.6) | copy-start | bytes 772
  76.4 17.5 %copy-start = (bf16[64,64,1024]{2,1,0:T(8,128)(2,1)S(1)}, bf16[64,64,1024]{2,1,0:T(8,128)(2,1)}, u32[]{:S(2)}) copy-start(bf16[64,64,1024]{2,1,0:T(8,128)(2,1)} %multiply_convert_fusion) | copy-start | bytes 25165828
  149.1 14.0 %copy-start.1 = (s32[1,64,2]{1,2,0:T(2,128)S(1)}, s32[1,64,2]{1,2,0:T(2,128)}, u32[]{:S(2)}) copy-start(s32[1,64,2]{1,2,0:T(2,128)} %param.8) | copy-start | bytes 1540
  149.1 199.1 %all-to-all-start = ((bf16[64,64,1,1024]{3,1,2,0:T(8,128)(2,1)}), bf16[64,64,1,1024]{3,1,2,0:T(8,128)(2,1)}, u32[]{:S(2)}, u32[]{:S(2)}) async-start(bf16[64,64,1,1024]{3,1,2,0:T(8,128)(2,1)} %constant_dynamic-update-slice_fusion), calls=%async_computation | async-start | bytes 16777216 | tf_op jit(solution)/shard_map/all_to_all | solution.py:21
  162.4 269.0 %reduce-scatter.2.cloned.1.call-start = ((), (), s32[]{:S(2)}) async-start(), calls=%async_computation.2 | async-start | bytes 5242880 | tf_op jit(solution)/shard_map/reduce_scatter | solution.py:48
Sparse Core Ops, SparseCore 0:
  385.2 46.1 reduce-scatter.1
